TPU v7x, 32 devices: a whole 2x2x4 slice. The times are simulated.
32 devices in a mesh: group: 2 (over y), replica: 16 (over z, x, core).
Axes of the slice: x: 2, y: 2, z: 4, core: 2. Of those that a mesh axis runs over, the one named last changes fastest.
Arguments:
- tokens: bfloat16 [6144, 960], P(('group', 'replica')), may hold values from -6 to 6
- seq_lens: int32 [32, 4], P(('group', 'replica')), may hold values from 1 to 96, 192 in all within a row
- cotangent: bfloat16 [6144, 960], P(('group', 'replica')), may hold values from -6 to 6
- norm1_gain: bfloat16 [960], P('group'), may hold values from 0.25 to 1.75
- w_query: bfloat16 [960, 960], P('group'), may hold values from -0.1875 to 0.1875
- key_weight: bfloat16 [960, 320], P('group'), may hold values from -0.1875 to 0.1875
- value_weight: bfloat16 [960, 320], P('group'), may hold values from -0.1875 to 0.1875
- w_output: bfloat16 [960, 960], P('group'), may hold values from -0.5 to 0.5
- norm2_gain: bfloat16 [960], P('group'), may hold values from 0.25 to 1.75
- w_gate: bfloat16 [960, 2560], P(None, 'group'), may hold values from -0.1875 to 0.1875
- w_up: bfloat16 [960, 2560], P(None, 'group'), may hold values from -0.1875 to 0.1875
- w_down: bfloat16 [2560, 960], P('group'), may hold values from -0.125 to 0.125
Outputs:
- layer_out: bfloat16 [6144, 960], P(('group', 'replica'))
- tokens_grad: float32 [6144, 960], P(('group', 'replica'))
- norm1_gain_grad: float32 [960], P('group')
- w_query_grad: float32 [960, 960], P('group')
- w_key_grad: float32 [960, 320], P('group')
- w_value_grad: float32 [960, 320], P('group')
- w_output_grad: float32 [960, 960], P('group')
- norm2_gain_grad: float32 [960], P('group')
- w_gate_grad: float32 [960, 2560], P(None, 'group')
- w_up_grad: float32 [960, 2560], P(None, 'group')
- w_down_grad: float32 [2560, 960], P('group')
Inputs may be any that keep to these rules, and one draw needn't show every extreme that they name: `seq_lens`: each device's row holds the lengths of its 4 sequences, which add up to 192; the longest in every row is 96.
All inputs are finite; a program needn't handle non-finite values.
Results may differ from a plain program's by a relative error of at most 0.023.
Values may be sent and summed in bfloat16 or wider, within the bound.
A program may use at most 192 MiB of HBM per device.

v0:
```python
import math
import jax
import jax.numpy as jnp
from jax import lax
from jax.sharding import PartitionSpec as P

QUERY_HEADS = 15
KEY_VALUE_HEADS = 5
HEAD_SIZE = 64
EPS = 1e-05


def matrix_product(left, right):
    return jnp.dot(left, right, preferred_element_type=jnp.float32)


def left_t_product(left, right):
    return lax.dot_general(
        left, right, (((0,), (0,)), ((), ())), preferred_element_type=jnp.float32
    )


def right_t_product(left, right):
    return lax.dot_general(
        left, right, (((1,), (1,)), ((), ())), preferred_element_type=jnp.float32
    )


def mixed_einsum(form, left, right):
    return jnp.einsum(form, left, right, preferred_element_type=jnp.float32)


def sequence_tables(lengths, token_count):
    ends = jnp.cumsum(lengths)
    starts = ends - lengths
    indices = jnp.arange(token_count, dtype=jnp.int32)
    seq_of = jnp.sum((indices[:, None] >= ends[None, :]).astype(jnp.int32), axis=1)
    onehot = (seq_of[:, None] == jnp.arange(lengths.shape[0], dtype=jnp.int32)[None, :]).astype(
        jnp.int32
    )
    position = indices - jnp.sum(onehot * starts[None, :], axis=1)
    half_dim = HEAD_SIZE // 2
    freqs = 10000.0 ** (-(jnp.arange(half_dim, dtype=jnp.float32) * 2.0 / HEAD_SIZE))
    angles = position.astype(jnp.float32)[:, None] * freqs[None, :]
    visible = (seq_of[:, None] == seq_of[None, :]) & (indices[None, :] <= indices[:, None])
    return (jnp.cos(angles), jnp.sin(angles), visible)


def apply_rotary(values, cosine_table, sine_table):
    half_dim = values.shape[-1] // 2
    first_half = values[..., :half_dim]
    second_half = values[..., half_dim:]
    cos_b = cosine_table[:, None, :]
    sin_b = sine_table[:, None, :]
    return jnp.concatenate(
        [first_half * cos_b - second_half * sin_b, second_half * cos_b + first_half * sin_b],
        axis=-1,
    )


def rotary_backward(values, cosine_table, sine_table):
    half_dim = values.shape[-1] // 2
    first_half = values[..., :half_dim]
    second_half = values[..., half_dim:]
    cos_b = cosine_table[:, None, :]
    sin_b = sine_table[:, None, :]
    return jnp.concatenate(
        [first_half * cos_b + second_half * sin_b, second_half * cos_b - first_half * sin_b],
        axis=-1,
    )


def rms_scale(resid, gain):
    inv_rms = lax.rsqrt(jnp.mean(resid * resid, axis=-1, keepdims=True) + EPS)
    return ((resid * inv_rms * gain.astype(jnp.float32)).astype(jnp.bfloat16), inv_rms)


def rms_back(d_normed, resid, inv_rms, gain):
    scaled = d_normed * gain.astype(jnp.float32)
    d_resid = inv_rms * scaled - resid * inv_rms**3 * jnp.mean(
        scaled * resid, axis=-1, keepdims=True
    )
    d_gain = jnp.sum(d_normed * resid * inv_rms, axis=0)
    return (d_resid, d_gain)


def masked_scores(query_rotated, key_rotated, visible):
    token_count = query_rotated.shape[0]
    query_grouped = query_rotated.reshape(
        token_count, KEY_VALUE_HEADS, QUERY_HEADS // KEY_VALUE_HEADS, HEAD_SIZE
    )
    scores = mixed_einsum("qhgd,khd->hgqk", query_grouped, key_rotated) * (
        1.0 / math.sqrt(HEAD_SIZE)
    )
    return (jnp.where(visible[None, None], scores, -1e30), query_grouped)


def attention(query_rotated, key_rotated, value_row_block, visible):
    token_count = query_rotated.shape[0]
    scores, query_grouped = masked_scores(query_rotated, key_rotated, visible)
    top = jnp.max(scores, axis=-1, keepdims=True)
    expo = jnp.exp(scores - top)
    total = jnp.sum(expo, axis=-1, keepdims=True)
    log_total = top + jnp.log(total)
    probs = (expo / total).astype(jnp.bfloat16)
    mixed = mixed_einsum("hgqk,khd->qhgd", probs, value_row_block)
    return (mixed.reshape(token_count, QUERY_HEADS * HEAD_SIZE).astype(jnp.bfloat16), log_total)


def attention_back(
    query_rotated,
    key_rotated,
    value_row_block,
    attention_mixture,
    mixture_gradient,
    log_total,
    visible,
):
    token_count = query_rotated.shape[0]
    scores, query_grouped = masked_scores(query_rotated, key_rotated, visible)
    weights_f = jnp.exp(scores - log_total)
    probs = weights_f.astype(jnp.bfloat16)
    mixture_gradient_grouped = mixture_gradient.reshape(
        token_count, KEY_VALUE_HEADS, QUERY_HEADS // KEY_VALUE_HEADS, HEAD_SIZE
    )
    mixture_grouped = attention_mixture.reshape(
        token_count, KEY_VALUE_HEADS, QUERY_HEADS // KEY_VALUE_HEADS, HEAD_SIZE
    )
    value_gradient = mixed_einsum("hgqk,qhgd->khd", probs, mixture_gradient_grouped)
    d_probs = mixed_einsum("qhgd,khd->hgqk", mixture_gradient_grouped, value_row_block)
    delta = mixed_einsum("qhgd,qhgd->hgq", mixture_gradient_grouped, mixture_grouped)[..., None]
    d_scores = (weights_f * (d_probs - delta) * (1.0 / math.sqrt(HEAD_SIZE))).astype(jnp.bfloat16)
    d_query = mixed_einsum("hgqk,khd->qhgd", d_scores, key_rotated).reshape(
        token_count, QUERY_HEADS, HEAD_SIZE
    )
    key_gradient = mixed_einsum("hgqk,qhgd->khd", d_scores, query_grouped)
    return (d_query, key_gradient, value_gradient)


def forward_pass(block, lengths, weights):
    gain_one, w_query, key_weight, value_weight, w_output, gain_two, w_gate, w_up, w_down = weights
    token_count = block.shape[0]
    cosine_table, sine_table, visible = sequence_tables(lengths, token_count)
    resid_in = block.astype(jnp.float32)
    first_normed_input, inv_rms_one = rms_scale(resid_in, gain_one)
    query_rotated = apply_rotary(
        matrix_product(first_normed_input, w_query).reshape(token_count, QUERY_HEADS, HEAD_SIZE),
        cosine_table,
        sine_table,
    ).astype(jnp.bfloat16)
    key_rotated = apply_rotary(
        matrix_product(first_normed_input, key_weight).reshape(
            token_count, KEY_VALUE_HEADS, HEAD_SIZE
        ),
        cosine_table,
        sine_table,
    ).astype(jnp.bfloat16)
    value_row_block = (
        matrix_product(first_normed_input, value_weight)
        .astype(jnp.bfloat16)
        .reshape(token_count, KEY_VALUE_HEADS, HEAD_SIZE)
    )
    attention_mixture, log_total = attention(query_rotated, key_rotated, value_row_block, visible)
    resid_mid = resid_in + matrix_product(attention_mixture, w_output)
    normed_two, inv_rms_two = rms_scale(resid_mid, gain_two)
    gate_pre = matrix_product(normed_two, w_gate)
    up_pre = matrix_product(normed_two, w_up)
    hidden = (jax.nn.silu(gate_pre) * up_pre).astype(jnp.bfloat16)
    resid_out = resid_mid + matrix_product(hidden, w_down)
    saved = (
        resid_in,
        first_normed_input,
        inv_rms_one,
        query_rotated,
        key_rotated,
        value_row_block,
        attention_mixture,
        log_total,
        resid_mid,
        normed_two,
        inv_rms_two,
        gate_pre,
        up_pre,
        hidden,
        cosine_table,
        sine_table,
        visible,
    )
    return (resid_out.astype(jnp.bfloat16), saved)


def mlp_backward(d_out, saved, weights):
    gain_one, w_query, key_weight, value_weight, w_output, gain_two, w_gate, w_up, w_down = weights
    resid_mid, normed_two, inv_rms_two, gate_pre, up_pre, hidden = saved[8:14]
    d_out_b = d_out.astype(jnp.bfloat16)
    grad_down = left_t_product(hidden, d_out_b)
    d_hidden = right_t_product(d_out_b, w_down)
    sigma = jax.nn.sigmoid(gate_pre)
    d_gate = (d_hidden * up_pre * sigma * (1.0 + gate_pre * (1.0 - sigma))).astype(jnp.bfloat16)
    d_up = (d_hidden * gate_pre * sigma).astype(jnp.bfloat16)
    grad_gate = left_t_product(normed_two, d_gate)
    grad_up = left_t_product(normed_two, d_up)
    d_normed_two = right_t_product(d_gate, w_gate) + right_t_product(d_up, w_up)
    d_resid_part, grad_gain_two = rms_back(d_normed_two, resid_mid, inv_rms_two, gain_two)
    return (d_out + d_resid_part, (grad_gain_two, grad_gate, grad_up, grad_down))


def attn_backward(d_resid_mid, saved, weights):
    gain_one, w_query, key_weight, value_weight, w_output, gain_two, w_gate, w_up, w_down = weights
    (
        resid_in,
        first_normed_input,
        inv_rms_one,
        query_rotated,
        key_rotated,
        value_row_block,
        attention_mixture,
        log_total,
    ) = saved[:8]
    cosine_table, sine_table, visible = saved[14:]
    token_count = resid_in.shape[0]
    d_mid_b = d_resid_mid.astype(jnp.bfloat16)
    grad_output = left_t_product(attention_mixture, d_mid_b)
    mixture_gradient = right_t_product(d_mid_b, w_output).astype(jnp.bfloat16)
    d_query, key_gradient, value_gradient = attention_back(
        query_rotated,
        key_rotated,
        value_row_block,
        attention_mixture,
        mixture_gradient,
        log_total,
        visible,
    )
    d_query_b = (
        rotary_backward(d_query, cosine_table, sine_table)
        .reshape(token_count, QUERY_HEADS * HEAD_SIZE)
        .astype(jnp.bfloat16)
    )
    key_gradient_block = (
        rotary_backward(key_gradient, cosine_table, sine_table)
        .reshape(token_count, KEY_VALUE_HEADS * HEAD_SIZE)
        .astype(jnp.bfloat16)
    )
    value_gradient_block = value_gradient.reshape(token_count, KEY_VALUE_HEADS * HEAD_SIZE).astype(
        jnp.bfloat16
    )
    grad_query = left_t_product(first_normed_input, d_query_b)
    grad_key = left_t_product(first_normed_input, key_gradient_block)
    grad_value = left_t_product(first_normed_input, value_gradient_block)
    d_normed_one = (
        right_t_product(d_query_b, w_query)
        + right_t_product(key_gradient_block, key_weight)
        + right_t_product(value_gradient_block, value_weight)
    )
    d_resid_part, grad_gain_one = rms_back(d_normed_one, resid_in, inv_rms_one, gain_one)
    return (
        d_resid_mid + d_resid_part,
        (grad_gain_one, grad_query, grad_key, grad_value, grad_output),
    )


def local(
    tokens,
    seq_lens,
    cotangent,
    norm1_gain,
    w_query,
    key_weight,
    value_weight,
    w_output,
    norm2_gain,
    w_gate,
    w_up,
    w_down,
):
    weights = (
        lax.all_gather(norm1_gain, "group", axis=0, tiled=True),
        lax.all_gather(w_query, "group", axis=0, tiled=True),
        lax.all_gather(key_weight, "group", axis=0, tiled=True),
        lax.all_gather(value_weight, "group", axis=0, tiled=True),
        lax.all_gather(w_output, "group", axis=0, tiled=True),
        lax.all_gather(norm2_gain, "group", axis=0, tiled=True),
        lax.all_gather(w_gate, "group", axis=1, tiled=True),
        lax.all_gather(w_up, "group", axis=1, tiled=True),
        lax.all_gather(w_down, "group", axis=0, tiled=True),
    )
    layer_out, saved = forward_pass(tokens, seq_lens[0], weights)
    weights = (
        lax.all_gather(norm1_gain, "group", axis=0, tiled=True),
        lax.all_gather(w_query, "group", axis=0, tiled=True),
        lax.all_gather(key_weight, "group", axis=0, tiled=True),
        lax.all_gather(value_weight, "group", axis=0, tiled=True),
        lax.all_gather(w_output, "group", axis=0, tiled=True),
        lax.all_gather(norm2_gain, "group", axis=0, tiled=True),
        lax.all_gather(w_gate, "group", axis=1, tiled=True),
        lax.all_gather(w_up, "group", axis=1, tiled=True),
        lax.all_gather(w_down, "group", axis=0, tiled=True),
    )
    factor = 1.0 / math.sqrt(
        float(tokens.shape[0] * lax.axis_size("group") * lax.axis_size("replica"))
    )
    d_resid_mid, mlp_grads = mlp_backward(cotangent.astype(jnp.float32), saved, weights)
    tokens_grad, attn_grads = attn_backward(d_resid_mid, saved, weights)
    parts = (
        lax.psum_scatter(
            attn_grads[0].astype(jnp.bfloat16), "group", scatter_dimension=0, tiled=True
        ).astype(jnp.float32),
        lax.psum_scatter(
            attn_grads[1].astype(jnp.bfloat16), "group", scatter_dimension=0, tiled=True
        ).astype(jnp.float32),
        lax.psum_scatter(
            attn_grads[2].astype(jnp.bfloat16), "group", scatter_dimension=0, tiled=True
        ).astype(jnp.float32),
        lax.psum_scatter(
            attn_grads[3].astype(jnp.bfloat16), "group", scatter_dimension=0, tiled=True
        ).astype(jnp.float32),
        lax.psum_scatter(
            attn_grads[4].astype(jnp.bfloat16), "group", scatter_dimension=0, tiled=True
        ).astype(jnp.float32),
        lax.psum_scatter(
            mlp_grads[0].astype(jnp.bfloat16), "group", scatter_dimension=0, tiled=True
        ).astype(jnp.float32),
        lax.psum_scatter(
            mlp_grads[1].astype(jnp.bfloat16), "group", scatter_dimension=1, tiled=True
        ).astype(jnp.float32),
        lax.psum_scatter(
            mlp_grads[2].astype(jnp.bfloat16), "group", scatter_dimension=1, tiled=True
        ).astype(jnp.float32),
        lax.psum_scatter(
            mlp_grads[3].astype(jnp.bfloat16), "group", scatter_dimension=0, tiled=True
        ).astype(jnp.float32),
    )
    totals = (
        lax.psum(parts[0].astype(jnp.bfloat16), "replica").astype(jnp.float32),
        lax.psum(parts[1].astype(jnp.bfloat16), "replica").astype(jnp.float32),
        lax.psum(parts[2].astype(jnp.bfloat16), "replica").astype(jnp.float32),
        lax.psum(parts[3].astype(jnp.bfloat16), "replica").astype(jnp.float32),
        lax.psum(parts[4].astype(jnp.bfloat16), "replica").astype(jnp.float32),
        lax.psum(parts[5].astype(jnp.bfloat16), "replica").astype(jnp.float32),
        lax.psum(parts[6].astype(jnp.bfloat16), "replica").astype(jnp.float32),
        lax.psum(parts[7].astype(jnp.bfloat16), "replica").astype(jnp.float32),
        lax.psum(parts[8].astype(jnp.bfloat16), "replica").astype(jnp.float32),
    )
    return (
        layer_out,
        tokens_grad,
        totals[0] * factor,
        totals[1] * factor,
        totals[2] * factor,
        totals[3] * factor,
        totals[4] * factor,
        totals[5] * factor,
        totals[6] * factor,
        totals[7] * factor,
        totals[8] * factor,
    )


def solution(mesh):
    in_specs = (
        P(("group", "replica"), None),
        P(("group", "replica"), None),
        P(("group", "replica"), None),
        P("group"),
        P("group", None),
        P("group", None),
        P("group", None),
        P("group", None),
        P("group"),
        P(None, "group"),
        P(None, "group"),
        P("group", None),
    )
    out_specs = (
        P(("group", "replica"), None),
        P(("group", "replica"), None),
        P("group"),
        P("group", None),
        P("group", None),
        P("group", None),
        P("group", None),
        P("group"),
        P(None, "group"),
        P(None, "group"),
        P("group", None),
    )
    return jax.shard_map(local, mesh=mesh, in_specs=in_specs, out_specs=out_specs, check_vma=False)
```

profile of v0, /device:TPU:0, one launch (start us, length us, event | category | flops | bytes accessed | tf_op | source)
XLA Modules:
  0.0 832.0 jit_solution(7892637476535821670)
XLA Ops:
  12.9 5.9 all-reduce.7
  18.8 17.0 %all-gather.1 = bf16[2,480,320]{1,2,0:T(8,128)(2,1)S(1)} all-gather(bf16[1,480,320]{1,2,0:T(8,128)(2,1)S(1)} %bitcast.134), channel_id=1, replica_groups=mesh['group'=2,'replica'=16] {'group'}, dimensions={0}, use_global_device_ids=true | all-gather | bytes 921600 | tf_op jit(solution)/shard_map/all_gather | solution.py:279
  37.1 17.9 %all-gather = bf16[2,480,320]{1,2,0:T(8,128)(2,1)S(1)} all-gather(bf16[1,480,320]{1,2,0:T(8,128)(2,1)S(1)} %bitcast.135), channel_id=1, replica_groups=mesh['group'=2,'replica'=16] {'group'}, dimensions={0}, use_global_device_ids=true | all-gather | bytes 921600 | tf_op jit(solution)/shard_map/all_gather | solution.py:280
  66.6 24.5 %all-gather.10.cloned.1.call-done = bf16[960,960]{1,0:T(8,128)(2,1)} async-done(((bf16[480,960]{1,0:T(8,128)(2,1)}), bf16[960,960]{1,0:T(8,128)(2,1)}) %all-gather.10.cloned.1.call-update) | async-done | bytes 1843216 | tf_op jit(solution)/shard_map/all_gather | solution.py:281
  95.3 62.2 %all-gather.14.cloned.1.call-done = bf16[960,2560]{1,0:T(8,128)(2,1)} async-done(((bf16[960,1280]{1,0:T(8,128)(2,1)}), bf16[960,2560]{1,0:T(8,128)(2,1)}) %all-gather.14.cloned.1.call-update) | async-done | bytes 4915216 | tf_op jit(solution)/shard_map/all_gather | solution.py:284
  157.5 5.0 fusion.46
  162.5 61.3 %all-gather.12.cloned.1.call-done = bf16[960,2560]{1,0:T(8,128)(2,1)} async-done(((bf16[960,1280]{1,0:T(8,128)(2,1)}), bf16[960,2560]{1,0:T(8,128)(2,1)}) %all-gather.12.cloned.1.call-update) | async-done | bytes 4915216 | tf_op jit(solution)/shard_map/all_gather | solution.py:283
  223.8 5.0 fusion.45
  228.8 61.3 %all-gather.16.cloned.1.call-done = bf16[2560,960]{0,1:T(8,128)(2,1)} async-done(((bf16[1280,960]{0,1:T(8,128)(2,1)}), bf16[2560,960]{0,1:T(8,128)(2,1)}) %all-gather.16.cloned.1.call-update) | async-done | bytes 4915216 | tf_op jit(solution)/shard_map/all_gather | solution.py:285
  290.1 6.4 multiply_convert_fusion
  298.2 4.8 multiply_reduce_fusion
  327.2 3.7 convolution_convert_fusion
  342.9 7.3 reduce-scatter.22.cloned.1.call-done
  352.0 31.5 %reduce-scatter.14.cloned.1.call-done = bf16[480,960]{1,0:T(8,128)(2,1)} async-done(((bf16[960,960]{1,0:T(8,128)(2,1)}), bf16[480,960]{1,0:T(8,128)(2,1)}) %reduce-scatter.14.cloned.1.call-update) | async-done | bytes 921616 | tf_op jit(solution)/shard_map/reduce_scatter | solution.py:317
  383.5 33.3 %reduce-scatter.12.cloned.1.call-done = bf16[480,960]{1,0:T(8,128)(2,1)} async-done(((bf16[960,960]{1,0:T(8,128)(2,1)}), bf16[480,960]{1,0:T(8,128)(2,1)}) %reduce-scatter.12.cloned.1.call-update) | async-done | bytes 921616 | tf_op jit(solution)/shard_map/reduce_scatter | solution.py:308
  416.8 65.0 %reduce-scatter.20.cloned.1.call-done = bf16[1280,960]{0,1:T(8,128)(2,1)} async-done(((bf16[2560,960]{0,1:T(8,128)(2,1)}), bf16[1280,960]{0,1:T(8,128)(2,1)}) %reduce-scatter.20.cloned.1.call-update) | async-done | bytes 2457616 | tf_op jit(solution)/shard_map/reduce_scatter | solution.py:329
  481.8 65.1 %reduce-scatter.18.cloned.1.call-done = bf16[960,1280]{1,0:T(8,128)(2,1)} async-done(((bf16[960,2560]{1,0:T(8,128)(2,1)}), bf16[960,1280]{1,0:T(8,128)(2,1)}) %reduce-scatter.18.cloned.1.call-update) | async-done | bytes 2457616 | tf_op jit(solution)/shard_map/reduce_scatter | solution.py:326
  546.9 65.0 %reduce-scatter.16.cloned.1.call-done = bf16[960,1280]{1,0:T(8,128)(2,1)} async-done(((bf16[960,2560]{1,0:T(8,128)(2,1)}), bf16[960,1280]{1,0:T(8,128)(2,1)}) %reduce-scatter.16.cloned.1.call-update) | async-done | bytes 2457616 | tf_op jit(solution)/shard_map/reduce_scatter | solution.py:323
  616.5 4.9 all-reduce.6
  621.6 33.8 %all-reduce.4 = (bf16[480]{0:T(512)(128)(2,1)S(1)}, bf16[480]{0:T(512)(128)(2,1)S(1)}) all-reduce(bf16[480]{0:T(512)(128)(2,1)S(1)} %dynamic-slice.3, bf16[480]{0:T(512)(128)(2,1)S(1)} %dynamic-slice.5), channel_id=1, replica_groups=mesh['group'=2,'replica'=16] {'replica'}, use_global_device_ids=true, to_apply=%region_11.12 | all-reduce | flops 960 | bytes 3840 | tf_op jit(solution)/shard_map/psum | solution.py:334
  657.1 5.1 fusion.10
  662.3 148.8 %all-reduce.10.cloned.1.call-done = (bf16[480,960]{1,0:T(8,128)(2,1)}, bf16[480,320]{0,1:T(8,128)(2,1)}, bf16[480,320]{0,1:T(8,128)(2,1)}, bf16[480,960]{1,0:T(8...) async-done(((bf16[480,960]{1,0:T(8,128)(2,1)}, bf16[480,320]{0,1:T(8,128)(2,1)}, bf16[480,320]{0,1:T(8,128)(2,1)}, ...) | async-done | bytes 9830416 | tf_op jit(solution)/shard_map/psum | solution.py:335
  811.1 4.5 convert_multiply_fusion
  820.7 4.7 convert_multiply_fusion.1
  (200 shorter events, 71.9 us)
Async XLA Ops:
  7.2 51.9 %all-gather.8.cloned.1.call-start = ((), (), s32[]{:S(2)}) async-start(), calls=%async_computation.7 | async-start | bytes 2949120 | tf_op jit(solution)/shard_map/all_gather | solution.py:278
  7.9 83.2 %all-gather.10.cloned.1.call-start = ((), (), s32[]{:S(2)}) async-start(), calls=%async_computation.8 | async-start | bytes 2949120 | tf_op jit(solution)/shard_map/all_gather | solution.py:281
  8.7 148.8 %all-gather.14.cloned.1.call-start = ((), (), s32[]{:S(2)}) async-start(), calls=%async_computation.10 | async-start | bytes 7372800 | tf_op jit(solution)/shard_map/all_gather | solution.py:284
  9.4 9.4 %copy-start.39 = (bf16[480,320]{0,1:T(8,128)(2,1)S(1)}, bf16[480,320]{0,1:T(8,128)(2,1)}, u32[]{:S(2)}) copy-start(bf16[480,320]{0,1:T(8,128)(2,1)} %param.17) | copy-start | bytes 921604
  9.5 214.3 %all-gather.12.cloned.1.call-start = ((), (), s32[]{:S(2)}) async-start(), calls=%async_computation.9 | async-start | bytes 7372800 | tf_op jit(solution)/shard_map/all_gather | solution.py:283
  10.0 27.1 %copy-start.40 = (bf16[480,320]{0,1:T(8,128)(2,1)S(1)}, bf16[480,320]{0,1:T(8,128)(2,1)}, u32[]{:S(2)}) copy-start(bf16[480,320]{0,1:T(8,128)(2,1)} %param.18) | copy-start | bytes 921604
  10.0 280.0 %all-gather.16.cloned.1.call-start = ((), (), s32[]{:S(2)}) async-start(), calls=%async_computation.11 | async-start | bytes 7372800 | tf_op jit(solution)/shard_map/all_gather | solution.py:285
  10.6 330.4 %reduce-scatter.24.cloned.1.call-start = ((), (), s32[]{:S(2)}) async-start(), calls=%async_computation.18 | async-start | bytes 1105920
  37.1 21.3 %copy-start.14 = (bf16[960,320]{0,1:T(8,128)(2,1)}, bf16[960,320]{0,1:T(8,128)(2,1)S(1)}, u32[]{:S(2)}) copy-start(bf16[960,320]{0,1:T(8,128)(2,1)S(1)} %reshape.227) | copy-start | bytes 1843204
  56.3 5.4 copy-start.16
  56.9 7.7 copy-start.36
  66.6 26.9 %copy-start.44 = (f32[5,3,192]{2,1,0:T(4,128)S(1)}, f32[5,3,192]{2,1,0:T(4,128)}, u32[]{:S(2)}) copy-start(f32[5,3,192]{2,1,0:T(4,128)} %copy-done.43) | copy-start | bytes 34564
  66.6 26.9 %copy-start.46 = (f32[5,3,192]{2,1,0:T(4,128)S(1)}, f32[5,3,192]{2,1,0:T(4,128)}, u32[]{:S(2)}) copy-start(f32[5,3,192]{2,1,0:T(4,128)} %copy-done.45) | copy-start | bytes 34564
  290.1 6.4 copy-start.2
  313.7 36.4 %reduce-scatter.22.cloned.1.call-start = ((), (), s32[]{:S(2)}) async-start(), calls=%async_computation.17 | async-start | bytes 1105920
  320.6 62.9 %reduce-scatter.14.cloned.1.call-start = ((), (), s32[]{:S(2)}) async-start(), calls=%async_computation.13 | async-start | bytes 2949120 | tf_op jit(solution)/shard_map/reduce_scatter | solution.py:317
  322.6 94.2 %reduce-scatter.12.cloned.1.call-start = ((), (), s32[]{:S(2)}) async-start(), calls=%async_computation.12 | async-start | bytes 2949120 | tf_op jit(solution)/shard_map/reduce_scatter | solution.py:308
  327.1 154.7 %reduce-scatter.20.cloned.1.call-start = ((), (), s32[]{:S(2)}) async-start(), calls=%async_computation.16 | async-start | bytes 7372800 | tf_op jit(solution)/shard_map/reduce_scatter | solution.py:329
  331.0 216.0 %reduce-scatter.18.cloned.1.call-start = ((), (), s32[]{:S(2)}) async-start(), calls=%async_computation.15 | async-start | bytes 7372800 | tf_op jit(solution)/shard_map/reduce_scatter | solution.py:326
  336.0 275.9 %reduce-scatter.16.cloned.1.call-start = ((), (), s32[]{:S(2)}) async-start(), calls=%async_computation.14 | async-start | bytes 7372800 | tf_op jit(solution)/shard_map/reduce_scatter | solution.py:323
  340.9 470.1 %all-reduce.10.cloned.1.call-start = ((), (), s32[]{:S(2)}) async-start(), calls=%async_computation.19 | async-start | bytes 19988480 | tf_op jit(solution)/shard_map/psum | solution.py:335
  615.8 41.3 %copy-start.9 = (f32[192,960]{1,0:T(8,128)S(1)}, f32[192,960]{1,0:T(8,128)}, u32[]{:S(2)}) copy-start(f32[192,960]{1,0:T(8,128)} %copy-done.7) | copy-start | bytes 2211844
  811.1 5.8 copy-start.27
  811.1 5.8 copy-start.28
  (41 other events, 93.9 us)
Sparse Core Ops, SparseCore 0:
  9.5 46.8 all-gather.7
  58.0 33.0 all-gather.9
  92.6 64.8 all-gather.13
  158.9 64.8 all-gather.11
  225.2 64.8 all-gather.15
  313.9 16.9 reduce-scatter.23
  333.1 16.9 reduce-scatter.21
  353.0 30.4 reduce-scatter.13
  386.3 30.4 reduce-scatter.11
  419.6 62.1 reduce-scatter.19
  484.7 62.1 reduce-scatter.17
  549.7 62.1 reduce-scatter.15
  616.7 194.3 all-reduce.9
where the time goes:
time: 833 us; the launch traced here: 832 us
  waiting for transfers between devices  628 us (75%)
  blocking collectives  79.5 us (10%)
  matrix products  63.8 us (8%)
  local copies, waits for them, and re-layouts  22.6 us (3%)
  other arithmetic  21.1 us (3%)
  between operations  16 us (2%)
    psum x1, waiting for transfers between devices, local(): lax.psum(parts[1].astype(jnp.bfloat16), 'replica').astype(jnp.float32)  149 us
    reduce_scatter x1, waiting for transfers between devices, local(): lax.psum_scatter(mlp_grads[2].astype(jnp.bfloat16), 'group', scatter_dime...  65.1 us
    reduce_scatter x1, waiting for transfers between devices, local(): lax.psum_scatter(mlp_grads[1].astype(jnp.bfloat16), 'group', scatter_dime...  65 us
    reduce_scatter x1, waiting for transfers between devices, local(): lax.psum_scatter(mlp_grads[3].astype(jnp.bfloat16), 'group', scatter_dime...  65 us
    all_gather x1, waiting for transfers between devices, local(): lax.all_gather(w_up, 'group', axis=1, tiled=True)  62.2 us
    all_gather x1, waiting for transfers between devices, local(): lax.all_gather(w_gate, 'group', axis=1, tiled=True)  61.3 us
    all_gather x1, waiting for transfers between devices, local(): lax.all_gather(w_down, 'group', axis=0, tiled=True)  61.3 us
    psum x1, blocking collectives, local(): lax.psum(parts[0].astype(jnp.bfloat16), 'replica').astype(jnp.float32)  33.8 us
  transfers between devices with their start and end apart: 13, of which 11 were waited for; matrix products, arithmetic and copies ran while one was open for 8% of the time, Pallas kernels for 0%

commit v1 on v0

--- a/solution.py
+++ b/solution.py
@@ -8,6 +8,11 @@
 KEY_VALUE_HEADS = 5
 HEAD_SIZE = 64
 EPS = 1e-05
+
+
+def gather_and_add(value, axis):
+    parts = lax.all_gather(value, axis)
+    return jnp.sum(parts, axis=0)
 
 
 def matrix_product(left, right):
@@ -332,7 +337,7 @@
     )
     totals = (
         lax.psum(parts[0].astype(jnp.bfloat16), "replica").astype(jnp.float32),
-        lax.psum(parts[1].astype(jnp.bfloat16), "replica").astype(jnp.float32),
+        gather_and_add(parts[1].astype(jnp.bfloat16), "replica").astype(jnp.float32),
         lax.psum(parts[2].astype(jnp.bfloat16), "replica").astype(jnp.float32),
         lax.psum(parts[3].astype(jnp.bfloat16), "replica").astype(jnp.float32),
         lax.psum(parts[4].astype(jnp.bfloat16), "replica").astype(jnp.float32),

time: 833 us -> 936 us (1.12)
  waiting for transfers between devices: 628 us -> 721 us
  other arithmetic: 21.1 us -> 30.6 us
    all_gather x0 -> x1, waiting for transfers between devices: none -> 108 us  [gather_and_add(): parts = lax.all_gather(value, axis)]
    psum x1, waiting for transfers between devices: 149 us -> 133 us  [local(): lax.psum(parts[2].astype(jnp.bfloat16), 'replica').astype(jnp.float32)]
    unnamed x117 -> x97, local copies, waits for them, and re-layouts: 19.1 us -> 19.7 us
  transfers between devices with their start and end apart: 13 -> 14, of which waited for: 11 -> 12; matrix products, arithmetic and copies ran while one was open for 8% -> 8% of each run, Pallas kernels for 0% -> 0%
where the time goes in v1:
time: 936 us; the launch traced here: 935 us
  waiting for transfers between devices  721 us (77%)
  blocking collectives  79.5 us (8%)
  matrix products  63.9 us (7%)
  other arithmetic  30.6 us (3%)
  local copies, waits for them, and re-layouts  23.8 us (3%)
  between operations  15.8 us (2%)
    psum x1, waiting for transfers between devices, local(): lax.psum(parts[2].astype(jnp.bfloat16), 'replica').astype(jnp.float32)  133 us
    all_gather x1, waiting for transfers between devices, gather_and_add(): parts = lax.all_gather(value, axis)  108 us
    reduce_scatter x1, waiting for transfers between devices, local(): lax.psum_scatter(mlp_grads[3].astype(jnp.bfloat16), 'group', scatter_dime...  65.1 us
    reduce_scatter x1, waiting for transfers between devices, local(): lax.psum_scatter(mlp_grads[1].astype(jnp.bfloat16), 'group', scatter_dime...  65.1 us
    reduce_scatter x1, waiting for transfers between devices, local(): lax.psum_scatter(mlp_grads[2].astype(jnp.bfloat16), 'group', scatter_dime...  65 us
    all_gather x1, waiting for transfers between devices, local(): lax.all_gather(w_up, 'group', axis=1, tiled=True)  62.2 us
    all_gather x1, waiting for transfers between devices, local(): lax.all_gather(w_gate, 'group', axis=1, tiled=True)  61.3 us
    all_gather x1, waiting for transfers between devices, local(): lax.all_gather(w_down, 'group', axis=0, tiled=True)  61.3 us
  transfers between devices with their start and end apart: 14, of which 12 were waited for; matrix products, arithmetic and copies ran while one was open for 8% of the time, Pallas kernels for 0%

profile of v1, /device:TPU:0, one launch (start us, length us, event | category | flops | bytes accessed | tf_op | source)
XLA Modules:
  0.0 934.7 jit_solution(11415830999854037372)
XLA Ops:
  12.9 5.9 all-reduce.7
  18.8 17.0 %all-gather.2 = bf16[2,480,320]{1,2,0:T(8,128)(2,1)S(1)} all-gather(bf16[1,480,320]{1,2,0:T(8,128)(2,1)S(1)} %bitcast.136), channel_id=1, replica_groups=mesh['group'=2,'replica'=16] {'group'}, dimensions={0}, use_global_device_ids=true | all-gather | bytes 921600 | tf_op jit(solution)/shard_map/all_gather | solution.py:284
  37.1 17.9 %all-gather.1 = bf16[2,480,320]{1,2,0:T(8,128)(2,1)S(1)} all-gather(bf16[1,480,320]{1,2,0:T(8,128)(2,1)S(1)} %bitcast.137), channel_id=1, replica_groups=mesh['group'=2,'replica'=16] {'group'}, dimensions={0}, use_global_device_ids=true | all-gather | bytes 921600 | tf_op jit(solution)/shard_map/all_gather | solution.py:285
  66.6 24.4 %all-gather.12.cloned.1.call-done = bf16[960,960]{1,0:T(8,128)(2,1)} async-done(((bf16[480,960]{1,0:T(8,128)(2,1)}), bf16[960,960]{1,0:T(8,128)(2,1)}) %all-gather.12.cloned.1.call-update) | async-done | bytes 1843216 | tf_op jit(solution)/shard_map/all_gather | solution.py:286
  95.3 62.2 %all-gather.16.cloned.1.call-done = bf16[960,2560]{1,0:T(8,128)(2,1)} async-done(((bf16[960,1280]{1,0:T(8,128)(2,1)}), bf16[960,2560]{1,0:T(8,128)(2,1)}) %all-gather.16.cloned.1.call-update) | async-done | bytes 4915216 | tf_op jit(solution)/shard_map/all_gather | solution.py:289
  157.5 5.0 fusion.46
  162.5 61.3 %all-gather.14.cloned.1.call-done = bf16[960,2560]{1,0:T(8,128)(2,1)} async-done(((bf16[960,1280]{1,0:T(8,128)(2,1)}), bf16[960,2560]{1,0:T(8,128)(2,1)}) %all-gather.14.cloned.1.call-update) | async-done | bytes 4915216 | tf_op jit(solution)/shard_map/all_gather | solution.py:288
  223.8 5.0 fusion.45
  228.8 61.3 %all-gather.18.cloned.1.call-done = bf16[2560,960]{0,1:T(8,128)(2,1)} async-done(((bf16[1280,960]{0,1:T(8,128)(2,1)}), bf16[2560,960]{0,1:T(8,128)(2,1)}) %all-gather.18.cloned.1.call-update) | async-done | bytes 4915216 | tf_op jit(solution)/shard_map/all_gather | solution.py:290
  290.1 6.4 multiply_convert_fusion
  298.1 4.2 multiply_reduce_fusion
  342.5 7.6 reduce-scatter.22.cloned.1.call-done
  352.0 31.5 %reduce-scatter.14.cloned.1.call-done = bf16[480,960]{1,0:T(8,128)(2,1)} async-done(((bf16[960,960]{1,0:T(8,128)(2,1)}), bf16[480,960]{1,0:T(8,128)(2,1)}) %reduce-scatter.14.cloned.1.call-update) | async-done | bytes 921616 | tf_op jit(solution)/shard_map/reduce_scatter | solution.py:322
  383.5 65.1 %reduce-scatter.20.cloned.1.call-done = bf16[1280,960]{0,1:T(8,128)(2,1)} async-done(((bf16[2560,960]{0,1:T(8,128)(2,1)}), bf16[1280,960]{0,1:T(8,128)(2,1)}) %reduce-scatter.20.cloned.1.call-update) | async-done | bytes 2457616 | tf_op jit(solution)/shard_map/reduce_scatter | solution.py:334
  448.6 65.0 %reduce-scatter.18.cloned.1.call-done = bf16[960,1280]{1,0:T(8,128)(2,1)} async-done(((bf16[960,2560]{1,0:T(8,128)(2,1)}), bf16[960,1280]{1,0:T(8,128)(2,1)}) %reduce-scatter.18.cloned.1.call-update) | async-done | bytes 2457616 | tf_op jit(solution)/shard_map/reduce_scatter | solution.py:331
  513.6 65.1 %reduce-scatter.16.cloned.1.call-done = bf16[960,1280]{1,0:T(8,128)(2,1)} async-done(((bf16[960,2560]{1,0:T(8,128)(2,1)}), bf16[960,1280]{1,0:T(8,128)(2,1)}) %reduce-scatter.16.cloned.1.call-update) | async-done | bytes 2457616 | tf_op jit(solution)/shard_map/reduce_scatter | solution.py:328
  578.8 33.1 %reduce-scatter.12.cloned.1.call-done = bf16[480,960]{1,0:T(8,128)(2,1)} async-done(((bf16[960,960]{1,0:T(8,128)(2,1)}), bf16[480,960]{1,0:T(8,128)(2,1)}) %reduce-scatter.12.cloned.1.call-update) | async-done | bytes 921616 | tf_op jit(solution)/shard_map/reduce_scatter | solution.py:313
  617.2 4.9 all-reduce.6
  622.3 33.8 %all-reduce.4 = (bf16[480]{0:T(512)(128)(2,1)S(1)}, bf16[480]{0:T(512)(128)(2,1)S(1)}) all-reduce(bf16[480]{0:T(512)(128)(2,1)S(1)} %dynamic-slice.3, bf16[480]{0:T(512)(128)(2,1)S(1)} %dynamic-slice.5), channel_id=1, replica_groups=mesh['group'=2,'replica'=16] {'replica'}, use_global_device_ids=true, to_apply=%region_11.12 | all-reduce | flops 960 | bytes 3840 | tf_op jit(solution)/shard_map/psum | solution.py:339
  657.8 5.1 fusion.10
  662.9 132.8 %all-reduce.10.cloned.1.call-done = (bf16[480,320]{0,1:T(8,128)(2,1)}, bf16[480,320]{0,1:T(8,128)(2,1)}, bf16[480,960]{1,0:T(8,128)(2,1)}, bf16[960,1280]{1,0:T(...) async-done(((bf16[480,320]{0,1:T(8,128)(2,1)}, bf16[480,320]{0,1:T(8,128)(2,1)}, bf16[480,960]{1,0:T(8,128)(2,1)}, bf16[960,1280]{1,0:T(8,128)(2,1)}, ...) | async-done | bytes 8908816 | tf_op jit(solution)/shard_map/psum | solution.py:341
  805.3 4.7 convert_multiply_fusion.1
  810.0 107.8 %all-gather.20.cloned.1.call-done = bf16[7680,960]{1,0:T(8,128)(2,1)} async-done(((bf16[480,960]{1,0:T(8,128)(2,1)}), bf16[7680,960]{1,0:T(8,128)(2,1)}) %all-gather.20.cloned.1.call-update) | async-done | bytes 14745616 | tf_op jit(solution)/shard_map/all_gather | solution.py:14
  917.8 8.8 reduce_sum.101
  (185 shorter events, 82.8 us)
Async XLA Ops:
  7.2 52.5 %all-gather.10.cloned.1.call-start = ((), (), s32[]{:S(2)}) async-start(), calls=%async_computation.7 | async-start | bytes 2949120 | tf_op jit(solution)/shard_map/all_gather | solution.py:283
  7.9 83.2 %all-gather.12.cloned.1.call-start = ((), (), s32[]{:S(2)}) async-start(), calls=%async_computation.8 | async-start | bytes 2949120 | tf_op jit(solution)/shard_map/all_gather | solution.py:286
  8.7 148.9 %all-gather.16.cloned.1.call-start = ((), (), s32[]{:S(2)}) async-start(), calls=%async_computation.10 | async-start | bytes 7372800 | tf_op jit(solution)/shard_map/all_gather | solution.py:289
  9.4 9.4 %copy-start.36 = (bf16[480,320]{0,1:T(8,128)(2,1)S(1)}, bf16[480,320]{0,1:T(8,128)(2,1)}, u32[]{:S(2)}) copy-start(bf16[480,320]{0,1:T(8,128)(2,1)} %param.17) | copy-start | bytes 921604
  9.5 214.3 %all-gather.14.cloned.1.call-start = ((), (), s32[]{:S(2)}) async-start(), calls=%async_computation.9 | async-start | bytes 7372800 | tf_op jit(solution)/shard_map/all_gather | solution.py:288
  10.0 27.1 %copy-start.37 = (bf16[480,320]{0,1:T(8,128)(2,1)S(1)}, bf16[480,320]{0,1:T(8,128)(2,1)}, u32[]{:S(2)}) copy-start(bf16[480,320]{0,1:T(8,128)(2,1)} %param.18) | copy-start | bytes 921604
  10.0 280.0 %all-gather.18.cloned.1.call-start = ((), (), s32[]{:S(2)}) async-start(), calls=%async_computation.11 | async-start | bytes 7372800 | tf_op jit(solution)/shard_map/all_gather | solution.py:290
  10.6 330.0 %reduce-scatter.24.cloned.1.call-start = ((), (), s32[]{:S(2)}) async-start(), calls=%async_computation.19 | async-start | bytes 1105920
  37.1 22.0 %copy-start.12 = (bf16[960,320]{0,1:T(8,128)(2,1)}, bf16[960,320]{0,1:T(8,128)(2,1)S(1)}, u32[]{:S(2)}) copy-start(bf16[960,320]{0,1:T(8,128)(2,1)S(1)} %reshape.228) | copy-start | bytes 1843204
  56.3 5.9 copy-start.14
  59.7 5.0 copy-start.32
  290.1 6.4 copy-start.2
  313.8 36.4 %reduce-scatter.22.cloned.1.call-start = ((), (), s32[]{:S(2)}) async-start(), calls=%async_computation.18 | async-start | bytes 1105920
  313.8 4.5 copy-start.28
  320.6 62.9 %reduce-scatter.14.cloned.1.call-start = ((), (), s32[]{:S(2)}) async-start(), calls=%async_computation.13 | async-start | bytes 2949120 | tf_op jit(solution)/shard_map/reduce_scatter | solution.py:322
  322.6 126.0 %reduce-scatter.20.cloned.1.call-start = ((), (), s32[]{:S(2)}) async-start(), calls=%async_computation.16 | async-start | bytes 7372800 | tf_op jit(solution)/shard_map/reduce_scatter | solution.py:334
  326.5 187.1 %reduce-scatter.18.cloned.1.call-start = ((), (), s32[]{:S(2)}) async-start(), calls=%async_computation.15 | async-start | bytes 7372800 | tf_op jit(solution)/shard_map/reduce_scatter | solution.py:331
  331.6 247.2 %reduce-scatter.16.cloned.1.call-start = ((), (), s32[]{:S(2)}) async-start(), calls=%async_computation.14 | async-start | bytes 7372800 | tf_op jit(solution)/shard_map/reduce_scatter | solution.py:328
  336.5 275.4 %reduce-scatter.12.cloned.1.call-start = ((), (), s32[]{:S(2)}) async-start(), calls=%async_computation.12 | async-start | bytes 2949120 | tf_op jit(solution)/shard_map/reduce_scatter | solution.py:313
  340.6 455.2 %all-reduce.10.cloned.1.call-start = ((), (), s32[]{:S(2)}) async-start(), calls=%async_computation.20 | async-start | bytes 18022400 | tf_op jit(solution)/shard_map/psum | solution.py:341
  578.7 36.2 %copy-start.13 = (bf16[960,320]{0,1:T(8,128)(2,1)S(1)}, bf16[960,320]{0,1:T(8,128)(2,1)}, u32[]{:S(2)}) copy-start(bf16[960,320]{0,1:T(8,128)(2,1)} %copy-done.12) | copy-start | bytes 1843204
  578.7 339.0 %all-gather.20.cloned.1.call-start = ((), (), s32[]{:S(2)}) async-start(), calls=%async_computation.17 | async-start | bytes 16711680 | tf_op jit(solution)/shard_map/all_gather | solution.py:14
  615.4 42.4 %copy-start.9 = (f32[192,960]{1,0:T(8,128)S(1)}, f32[192,960]{1,0:T(8,128)}, u32[]{:S(2)}) copy-start(f32[192,960]{1,0:T(8,128)} %copy-done.7) | copy-start | bytes 2211844
  795.8 5.2 copy-start.17
  (32 other events, 65.9 us)
Sparse Core Ops, SparseCore 0:
  9.5 46.8 all-gather.9
  58.0 33.0 all-gather.11
  92.6 64.8 all-gather.15
  158.9 64.8 all-gather.13
  225.2 64.8 all-gather.17
  313.9 16.9 reduce-scatter.23
  333.1 16.9 reduce-scatter.21
  353.0 30.4 reduce-scatter.13
  386.4 62.1 reduce-scatter.19
  451.3 62.1 reduce-scatter.17
  516.5 62.1 reduce-scatter.15
  581.4 30.4 reduce-scatter.11
  616.4 179.2 all-reduce.9
  797.9 119.8 all-gather.19
